TPU v7x, 32 devices: a whole 2x2x4 slice. The times are simulated.
32 devices in a mesh: dp: 4 (over y, x), wide: 8 (over z, core).
Axes of the slice: x: 2, y: 2, z: 4, core: 2. Of those that a mesh axis runs over, the one named last changes fastest.
Arguments:
- clips: bfloat16 [4, 8, 4, 128, 512], P('dp', 'wide'), may hold values from -8 to 8
- w_spatial: bfloat16 [4608, 512], P(None, 'dp'), may hold values from -0.09375 to 0.09375
- w_time: bfloat16 [1536, 512], replicated, may hold values from -0.15625 to 0.15625
- norm_gain: float32 [512], replicated, may hold values from 0.1 to 1.9
- norm_bias: float32 [512], replicated, may hold values from -0.6 to 0.6
- grad_out: bfloat16 [4, 8, 512, 512], P('dp', None, 'wide'), may hold values from -6 to 6
Outputs:
- grad_clips: bfloat16 [4, 8, 4, 128, 512], P('dp', 'wide')
- spatial_grad: float32 [4608, 512], P('dp', 'wide')
- time_grad: float32 [1536, 512], P('dp', 'wide')
All inputs are finite; a program needn't handle non-finite values.
Results may differ from a plain program's by a relative error of at most 0.009.
Values may be sent and summed in bfloat16 or wider, within the bound.
No kernel may reach another device: no remote copies, remote signals or barrier semaphores. Data moves between devices by JAX's collectives and lax.ppermute only.
A program may use at most 128 MiB of HBM per device.

v0:
```python
import jax
import jax.numpy as jnp
from jax import lax
from jax.sharding import PartitionSpec as P

G = 32
FRAMES = 8
EPSILON = 1e-06
CONTRACT_ROWS = (((0,), (0,)), ((), ()))
CONTRACT_COLS = (((1,), (1,)), ((), ()))


def pad_frames(frames):
    return jnp.pad(frames, ((0, 0), (1, 1), (1, 1), (0, 0)))


def spatial_forward(frames, weights):
    frame_total, row_count, col_count, chan_count = frames.shape
    padded = pad_frames(frames)
    accum_out = jnp.zeros((frame_total * row_count * col_count, weights.shape[1]), jnp.float32)
    for tap_index in range(9):
        row_off, col_off = (tap_index // 3, tap_index % 3)
        window = padded[:, row_off : row_off + row_count, col_off : col_off + col_count, :].reshape(
            -1, chan_count
        )
        tap_weight = weights[tap_index * chan_count : (tap_index + 1) * chan_count]
        accum_out = accum_out + jnp.dot(window, tap_weight, preferred_element_type=jnp.float32)
    return accum_out.reshape(frame_total, row_count, col_count, -1)


def spatial_backward(frames, grad_hidden, weights):
    frame_total, row_count, col_count, chan_count = frames.shape
    padded_in = pad_frames(frames)
    padded_grad = pad_frames(grad_hidden)
    grad_flat = grad_hidden.reshape(-1, chan_count)
    grad_input = jnp.zeros((frame_total * row_count * col_count, chan_count), jnp.float32)
    tap_grads = []
    for tap_index in range(9):
        row_off, col_off = (tap_index // 3, tap_index % 3)
        window = padded_in[
            :, row_off : row_off + row_count, col_off : col_off + col_count, :
        ].reshape(-1, chan_count)
        tap_grads.append(
            lax.dot_general(window, grad_flat, CONTRACT_ROWS, preferred_element_type=jnp.float32)
        )
        flipped = padded_grad[
            :, 2 - row_off : 2 - row_off + row_count, 2 - col_off : 2 - col_off + col_count, :
        ].reshape(-1, chan_count)
        tap_weight = weights[tap_index * chan_count : (tap_index + 1) * chan_count]
        grad_input = grad_input + lax.dot_general(
            flipped, tap_weight, CONTRACT_COLS, preferred_element_type=jnp.float32
        )
    return (grad_input.reshape(frames.shape), jnp.concatenate(tap_grads, axis=0))


def norm_forward(hidden, norm_gain, norm_bias):
    frame_total, row_count, col_count, chan_count = hidden.shape
    grouped = hidden.astype(jnp.float32).reshape(
        frame_total, row_count * col_count, G, chan_count // G
    )
    group_mean = jnp.mean(grouped, axis=(1, 3), keepdims=True)
    centered = grouped - group_mean
    variance = jnp.mean(centered * centered, axis=(1, 3), keepdims=True)
    inv_std = lax.rsqrt(variance + EPSILON)
    normed = centered * inv_std
    preact = normed.reshape(hidden.shape) * norm_gain + norm_bias
    return (preact, normed, inv_std)


def norm_backward(grad_act, preact, normed, inv_std, norm_gain):
    sigmoid_z = jax.nn.sigmoid(preact)
    grad_pre = grad_act.astype(jnp.float32) * sigmoid_z * (1.0 + preact * (1.0 - sigmoid_z))
    grad_normed = (grad_pre * norm_gain).reshape(normed.shape)
    mean_grad = jnp.mean(grad_normed, axis=(1, 3), keepdims=True)
    mean_proj = jnp.mean(grad_normed * normed, axis=(1, 3), keepdims=True)
    return ((grad_normed - mean_grad - normed * mean_proj) * inv_std).reshape(preact.shape)


def temporal_backward(tiles, grad_out, w_time):
    clip_count, frame_total, pix_count, chan_count = tiles.shape
    grad_act = jnp.zeros(tiles.shape, jnp.float32)
    tap_grads = []
    for tap_index in range(3):
        kept = frame_total - tap_index
        earlier = tiles[:, :kept].reshape(-1, chan_count)
        later = grad_out[:, tap_index:].reshape(-1, chan_count)
        tap_grads.append(
            lax.dot_general(earlier, later, CONTRACT_ROWS, preferred_element_type=jnp.float32)
        )
        tap_weight = w_time[tap_index * chan_count : (tap_index + 1) * chan_count]
        back_part = lax.dot_general(
            later, tap_weight, CONTRACT_COLS, preferred_element_type=jnp.float32
        )
        back_part = back_part.reshape(clip_count, kept, pix_count, chan_count)
        grad_act = grad_act + jnp.pad(back_part, ((0, 0), (0, tap_index), (0, 0), (0, 0)))
    return (jnp.concatenate(tap_grads, axis=0), grad_act)


def shards(clips, w_spatial, w_time, norm_gain, norm_bias, grad_out):
    group_count, frame_count, row_count, col_count, chan_count = clips.shape
    frames = clips.reshape(group_count * frame_count, row_count, col_count, chan_count)
    weights = lax.all_gather(w_spatial, "dp", axis=1, tiled=True)
    hidden = spatial_forward(frames, weights).astype(jnp.bfloat16)
    preact, normed, inv_std = norm_forward(hidden, norm_gain, norm_bias)
    act = (
        jax.nn.silu(preact)
        .astype(jnp.bfloat16)
        .reshape(group_count, frame_count, row_count * col_count, chan_count)
    )
    tiles = lax.all_to_all(act, "wide", split_axis=2, concat_axis=1, tiled=True)
    tile_shape = tiles.shape
    by_clip = tiles.reshape(-1, FRAMES, tile_shape[2], tile_shape[3])
    grad_clipwise = grad_out.reshape(by_clip.shape)
    time_raw, grad_act = temporal_backward(by_clip, grad_clipwise, w_time)
    grad_act = grad_act.astype(jnp.bfloat16).reshape(tile_shape)
    returned = lax.all_to_all(grad_act, "wide", split_axis=1, concat_axis=2, tiled=True)
    grad_hidden = norm_backward(
        returned.reshape(frames.shape), preact, normed, inv_std, norm_gain
    ).astype(jnp.bfloat16)
    grad_input, spatial_raw = spatial_backward(frames, grad_hidden, weights)
    position_total = (
        group_count
        * frame_count
        * row_count
        * col_count
        * lax.axis_size("wide")
        * lax.axis_size("dp")
    )
    grad_scale = float(position_total) ** (-0.5)
    partial_pair = (
        lax.psum_scatter(spatial_raw, "wide", scatter_dimension=1, tiled=True),
        lax.psum_scatter(time_raw, "wide", scatter_dimension=1, tiled=True),
    )
    spatial_sum, time_sum = (
        lax.psum_scatter(partial_pair[0], "dp", scatter_dimension=0, tiled=True),
        lax.psum_scatter(partial_pair[1], "dp", scatter_dimension=0, tiled=True),
    )
    grad_clips = grad_input.astype(jnp.bfloat16).reshape(clips.shape)
    return (grad_clips, spatial_sum * grad_scale, time_sum * grad_scale)


def solution(mesh):
    return jax.shard_map(
        shards,
        mesh=mesh,
        in_specs=(
            P("dp", "wide", None, None, None),
            P(None, "dp"),
            P(),
            P(),
            P(),
            P("dp", None, "wide", None),
        ),
        out_specs=(P("dp", "wide", None, None, None), P("dp", "wide"), P("dp", "wide")),
        check_vma=False,
    )
```

profile of v0, /device:TPU:0, one launch (start us, length us, event | category | flops | bytes accessed | tf_op | source)
XLA Modules:
  0.0 337.8 jit_solution(4861131859740784181)
XLA Ops:
  9.5 1.6 convolution_bitcast_fusion.12
  11.1 2.3 fusion.15
  13.4 6.4 %all-to-all-start = ((bf16[1,8,64,512]{3,2,0,1:T(8,128)(2,1)}), bf16[1,8,64,512]{3,2,0,1:T(8,128)(2,1)S(1)}, u32[]{:S(2)}, u32[]{:S(2)}) async-start(bf16[1,8,64,512]{3,2,0,1:T(8,128)(2,1)} %fusion.15), calls=%async_computation | async-start | bytes 1048576 | tf_op jit(solution)/shard_map/all_to_all | solution.py:116
  20.1 2.5 pad_slice_fusion
  22.6 2.1 copy.46
  24.7 2.0 copy.40
  26.7 2.1 copy.41
  28.8 2.0 copy.42
  30.8 2.0 copy.43
  32.9 2.0 copy.44
  36.9 32.4 %all-gather.2.cloned.1.call-done = bf16[4608,512]{1,0:T(8,128)(2,1)} async-done(((bf16[4608,128]{1,0:T(8,128)(2,1)}), bf16[4608,512]{1,0:T(8,128)(2,1)}) %all-gather.2.cloned.1.call-update) | async-done | bytes 4718608 | tf_op jit(solution)/shard_map/all_gather | solution.py:102
  69.4 1.8 fusion.58
  71.2 1.6 convolution_add_fusion.15
  77.0 1.6 fusion.68
  80.1 1.8 copy.58
  82.4 5.6 %reduce.16 = bf16[512,512]{1,0:T(8,128)(2,1)} reduce(bf16[512,1,1,512]{3,2,1,0:T(2,128)(2,1)} %bitcast.222, bf16[]{:T(256)} %broadcast.543), dimensions={1,2}, to_apply=%bitcast.194.reduce_sub_computation | reduce | bytes 1048578
  88.0 2.2 reshape.596
  90.2 20.0 %all_to_all.21 = bf16[8,2,16384]{2,1,0:T(2,128)(2,1)} all-to-all(bf16[8,2,16384]{2,1,0:T(2,128)(2,1)} %reshape.596), channel_id=1, replica_groups=mesh['dp'=4,'wide'=8] {'wide'}, dimensions={0} | all-to-all | bytes 1048576 | tf_op jit(solution)/shard_map/all_to_all | solution.py:110
  110.2 3.5 %reshape.597 = bf16[512,1,1,512]{3,2,1,0:T(2,128)(2,1)} reshape(bf16[8,2,16384]{2,1,0:T(2,128)(2,1)} %all_to_all.21) | data formatting | bytes 1048576
  116.4 2.0 pad_maximum_fusion
  118.4 3.6 %copy.53 = f32[1536,512]{0,1:T(8,128)} copy(f32[1536,512]{1,0:T(8,128)} %pad_maximum_fusion) | data formatting | bytes 6291456
  136.8 9.7 %copy.51 = f32[4608,512]{0,1:T(8,128)} copy(f32[4608,512]{1,0:T(8,128)} %fusion) | data formatting | bytes 18874368
  146.6 13.9 %reduce-scatter.15.cloned.1.call-done = f32[64,1536]{1,0:T(8,128)} async-done(((f32[512,1536]{1,0:T(8,128)}), f32[64,1536]{1,0:T(8,128)}) %reduce-scatter.15.cloned.1.call-update) | async-done | bytes 393232
  160.5 2.2 copy.54
  163.4 1.9 pad_slice_fusion.8
  166.8 94.7 %reduce-scatter.13.cloned.1.call-done = f32[64,4608]{1,0:T(8,128)} async-done(((f32[512,4608]{1,0:T(8,128)}), f32[64,4608]{1,0:T(8,128)}) %reduce-scatter.13.cloned.1.call-update) | async-done | bytes 1179664
  261.5 2.9 copy.52
  264.5 1.8 convolution_add_fusion.7
  266.3 1.7 convolution_add_fusion.6
  268.1 1.7 convolution_add_fusion.5
  273.1 15.9 %reduce-scatter.11.cloned.1.call-done = f32[384,64]{1,0:T(8,128)} async-done(((f32[1536,64]{1,0:T(8,128)}), f32[384,64]{1,0:T(8,128)}) %reduce-scatter.11.cloned.1.call-update) | async-done | bytes 98320 | tf_op jit(solution)/shard_map/reduce_scatter | solution.py:136
  290.6 38.6 %reduce-scatter.9.cloned.1.call-done = f32[1152,64]{1,0:T(8,128)} async-done(((f32[4608,64]{1,0:T(8,128)}), f32[1152,64]{1,0:T(8,128)}) %reduce-scatter.9.cloned.1.call-update) | async-done | bytes 294928 | tf_op jit(solution)/shard_map/reduce_scatter | solution.py:135
  (107 shorter events, 37.4 us)
Async XLA Ops:
  7.2 3.9 %copy-start.1 = (bf16[1,8,64,512]{3,2,1,0:T(8,128)(2,1)S(1)}, bf16[1,8,64,512]{3,2,1,0:T(8,128)(2,1)}, u32[]{:S(2)}) copy-start(bf16[1,8,64,512]{3,2,1,0:T(8,128)(2,1)} %param.11) | copy-start | bytes 1572868
  7.2 12.6 %copy-start.2 = (bf16[1,1,4,128,512]{4,3,2,1,0:T(8,128)(2,1)S(1)}, bf16[1,1,4,128,512]{4,3,2,1,0:T(8,128)(2,1)}, u32[]{:S(2)}) copy-start(bf16[1,1,4,128,512]{4,3,2,1,0:T(8,128)(2,1)} %param.6) | copy-start | bytes 1572868
  7.2 62.2 %all-gather.2.cloned.1.call-start = ((), (), s32[]{:S(2)}) async-start(), calls=%async_computation.6 | async-start | bytes 5898240 | tf_op jit(solution)/shard_map/all_gather | solution.py:102
  13.4 63.6 %all-to-all-start = ((bf16[1,8,64,512]{3,2,0,1:T(8,128)(2,1)}), bf16[1,8,64,512]{3,2,0,1:T(8,128)(2,1)S(1)}, u32[]{:S(2)}, u32[]{:S(2)}) async-start(bf16[1,8,64,512]{3,2,0,1:T(8,128)(2,1)} %fusion.15), calls=%async_computation | async-start | bytes 1048576 | tf_op jit(solution)/shard_map/all_to_all | solution.py:116
  19.8 140.7 %reduce-scatter.15.cloned.1.call-start = ((), (), s32[]{:S(2)}) async-start(), calls=%async_computation.10 | async-start | bytes 3538944
  35.9 37.4 %copy-start.12 = (bf16[1,4,128,512]{3,2,1,0:T(8,128)(2,1)S(1)}, bf16[1,4,128,512]{3,2,1,0:T(8,128)(2,1)}, u32[]{:S(2)}) copy-start(bf16[1,4,128,512]{3,2,1,0:T(8,128)(2,1)} %copy.42) | copy-start | bytes 1572868
  36.9 35.9 %copy-start.13 = (bf16[1,4,128,512]{3,2,1,0:T(8,128)(2,1)S(1)}, bf16[1,4,128,512]{3,2,1,0:T(8,128)(2,1)}, u32[]{:S(2)}) copy-start(bf16[1,4,128,512]{3,2,1,0:T(8,128)(2,1)} %copy.41) | copy-start | bytes 1572868
  69.4 3.4 %copy-start = (bf16[4608,512]{1,0:T(8,128)(2,1)S(1)}, bf16[4608,512]{1,0:T(8,128)(2,1)}, u32[]{:S(2)}) copy-start(bf16[4608,512]{1,0:T(8,128)(2,1)} %all-gather.2.cloned.1.call-done) | copy-start | bytes 14155780
  72.8 1.4 copy-start.11
  73.3 1.4 copy-start.10
  73.7 1.4 copy-start.9
  74.2 1.4 copy-start.8
  74.7 2.3 copy-start.14
  74.7 2.3 copy-start.15
  122.0 139.5 %reduce-scatter.13.cloned.1.call-start = ((), (), s32[]{:S(2)}) async-start(), calls=%async_computation.9 | async-start | bytes 10616832
  123.5 5.9 %copy-start.3 = (bf16[1,1,4,128,512]{4,3,2,1,0:T(8,128)(2,1)S(1)}, bf16[1,1,4,128,512]{4,3,2,1,0:T(8,128)(2,1)}, u32[]{:S(2)}) copy-start(bf16[1,1,4,128,512]{4,3,2,1,0:T(8,128)(2,1)} %param.6) | copy-start | bytes 1572868
  146.5 142.4 %reduce-scatter.11.cloned.1.call-start = ((), (), s32[]{:S(2)}) async-start(), calls=%async_computation.8 | async-start | bytes 983040 | tf_op jit(solution)/shard_map/reduce_scatter | solution.py:136
  162.7 166.6 %reduce-scatter.9.cloned.1.call-start = ((), (), s32[]{:S(2)}) async-start(), calls=%async_computation.7 | async-start | bytes 2949120 | tf_op jit(solution)/shard_map/reduce_scatter | solution.py:135
  261.5 8.3 %slice-start = ((s8[4718592]{0:T(1024)(128)(4,1)}), s8[524288]{0:T(1024)(128)(4,1)S(1)}, s32[]{:S(2)}) async-start(s8[4718592]{0:T(1024)(128)(4,1)} %bitcast.214), calls=%async_computation.11 | async-start | bytes 1048576
  264.5 5.3 %slice-start.1 = ((s8[4718592]{0:T(1024)(128)(4,1)}), s8[4194304]{0:T(1024)(128)(4,1)S(1)}, s32[]{:S(2)}) async-start(s8[4718592]{0:T(1024)(128)(4,1)} %bitcast.214), calls=%async_computation.12 | async-start | bytes 8388608
  266.3 4.0 %copy-start.7 = (bf16[1,4,128,512]{3,2,1,0:T(8,128)(2,1)S(1)}, bf16[1,4,128,512]{3,2,1,0:T(8,128)(2,1)}, u32[]{:S(2)}) copy-start(bf16[1,4,128,512]{3,2,1,0:T(8,128)(2,1)} %get-tuple-element.24) | copy-start | bytes 1572868
  268.0 2.8 copy-start.6
  269.8 1.5 copy-start.5
  270.3 1.5 copy-start.4
Sparse Core Ops, SparseCore 0:
  9.8 59.5 all-gather.1
  122.1 38.3 reduce-scatter.14
  162.8 98.6 reduce-scatter.12
  264.3 24.6 reduce-scatter.10
  291.8 37.3 reduce-scatter.8
where the time goes:
time: 339 us; the launch traced here: 338 us
  waiting for transfers between devices  196 us (58%)
  local copies, waits for them, and re-layouts  49.4 us (15%)
  matrix products  36.5 us (11%)
  blocking collectives  20 us (6%)
  other arithmetic  14.8 us (4%)
  between operations  14.3 us (4%)
  starting transfers between devices  6.55 us (2%)
    unnamed x7, waiting for transfers between devices  109 us
    reduce_scatter x1, waiting for transfers between devices, shards(): lax.psum_scatter(partial_pair[0], 'dp', scatter_dimension=0, tiled=True)  38.6 us
    all_gather x1, waiting for transfers between devices, shards(): weights = lax.all_gather(w_spatial, 'dp', axis=1, tiled=True)  32.4 us
    unnamed x47, local copies, waits for them, and re-layouts  27.9 us
    all_to_all x1, blocking collectives, shards(): tiles = lax.all_to_all(act, 'wide', split_axis=2, concat_axis=1, tiled=True)  20 us
    slice x9, local copies, waits for them, and re-layouts, spatial_forward(): padded[:, row_off:row_off + row_count, col_off:col_off + col_count, :]  16.8 us
    reduce_scatter x1, waiting for transfers between devices, shards(): lax.psum_scatter(partial_pair[1], 'dp', scatter_dimension=0, tiled=True)  15.9 us
    dot_general x9, matrix products, spatial_backward(): lax.dot_general(window, grad_flat, CONTRACT_ROWS, preferred_element_type=...  13.3 us
  transfers between devices with their start and end apart: 6, of which 5 were waited for; matrix products, arithmetic and copies ran while one was open for 22% of the time, Pallas kernels for 0%

commit v1 on v0

--- a/solution.py
+++ b/solution.py
@@ -99,7 +99,14 @@
 def shards(clips, w_spatial, w_time, norm_gain, norm_bias, grad_out):
     group_count, frame_count, row_count, col_count, chan_count = clips.shape
     frames = clips.reshape(group_count * frame_count, row_count, col_count, chan_count)
-    weights = lax.all_gather(w_spatial, "dp", axis=1, tiled=True)
+    ways, here, step = (lax.axis_size("dp"), lax.axis_index("dp"), w_spatial.shape[1])
+    line, have = (w_spatial, 1)
+    while have < ways:
+        line = jnp.concatenate(
+            [line, lax.ppermute(line, "dp", [(d, (d - have) % ways) for d in range(ways)])], axis=1
+        )
+        have = 2 * have
+    weights = jnp.roll(line, here * step, axis=1)
     hidden = spatial_forward(frames, weights).astype(jnp.bfloat16)
     preact, normed, inv_std = norm_forward(hidden, norm_gain, norm_bias)
     act = (

time: 339 us -> 368 us (1.086)
  local copies, waits for them, and re-layouts: 49.4 us -> 58.3 us
  waiting for transfers between devices: 196 us -> 204 us
  starting transfers between devices: 6.55 us -> 10.5 us
  matrix products: 36.5 us -> 40.3 us
    ppermute x0 -> x2, waiting for transfers between devices: none -> 44.4 us  [shards(): lax.ppermute(line, 'dp', [(d, (d - have) % ways) for d in range(ways)])]
    all_gather x1 -> x0, waiting for transfers between devices: 32.4 us -> none  [shards(): weights = lax.all_gather(w_spatial, 'dp', axis=1, tiled=True)]
    dot_general x9, matrix products: 9.93 us -> 15.4 us  [spatial_backward(): lax.dot_general(flipped, tap_weight, CONTRACT_COLS, preferred_element_typ...]
    ppermute x0 -> x2, starting transfers between devices: none -> 5.42 us  [shards(): lax.ppermute(line, 'dp', [(d, (d - have) % ways) for d in range(ways)])]
    reduce_scatter x1, waiting for transfers between devices: 15.9 us -> 10.7 us  [shards(): lax.psum_scatter(partial_pair[1], 'dp', scatter_dimension=0, tiled=True)]
    unnamed x47 -> x48, local copies, waits for them, and re-layouts: 27.9 us -> 32.5 us
    unnamed x7 -> x6, waiting for transfers between devices: 109 us -> 111 us
  transfers between devices with their start and end apart: 6 -> 7, of which waited for: 5 -> 6; matrix products, arithmetic and copies ran while one was open for 22% -> 24% of each run, Pallas kernels for 0% -> 0%
where the time goes in v1:
time: 368 us; the launch traced here: 366 us
  waiting for transfers between devices  204 us (55%)
  local copies, waits for them, and re-layouts  58.3 us (16%)
  matrix products  40.3 us (11%)
  blocking collectives  20.3 us (6%)
  other arithmetic  17.9 us (5%)
  between operations  14.2 us (4%)
  starting transfers between devices  10.5 us (3%)
    unnamed x6, waiting for transfers between devices  111 us
    ppermute x2, waiting for transfers between devices, shards(): lax.ppermute(line, 'dp', [(d, (d - have) % ways) for d in range(ways)])  44.4 us
    reduce_scatter x1, waiting for transfers between devices, shards(): lax.psum_scatter(partial_pair[0], 'dp', scatter_dimension=0, tiled=True)  38.6 us
    unnamed x48, local copies, waits for them, and re-layouts  32.5 us
    all_to_all x1, blocking collectives, shards(): tiles = lax.all_to_all(act, 'wide', split_axis=2, concat_axis=1, tiled=True)  20.3 us
    slice x9, local copies, waits for them, and re-layouts, spatial_forward(): padded[:, row_off:row_off + row_count, col_off:col_off + col_count, :]  19.4 us
    dot_general x9, matrix products, spatial_backward(): lax.dot_general(flipped, tap_weight, CONTRACT_COLS, preferred_element_typ...  15.4 us
    dot_general x9, matrix products, spatial_backward(): lax.dot_general(window, grad_flat, CONTRACT_ROWS, preferred_element_type=...  13.3 us
  transfers between devices with their start and end apart: 7, of which 6 were waited for; matrix products, arithmetic and copies ran while one was open for 24% of the time, Pallas kernels for 0%

profile of v1, /device:TPU:0, one launch (start us, length us, event | category | flops | bytes accessed | tf_op | source)
XLA Modules:
  0.0 366.0 jit_solution(153292731527029675)
XLA Ops:
  7.2 4.0 %collective-permute-start = (bf16[4608,128]{1,0:T(8,128)(2,1)}, bf16[4608,128]{1,0:T(8,128)(2,1)S(1)}, u32[]{:S(2)}, u32[]{:S(2)}) collective-permute-start(bf16[4608,128]{1,0:T(8,128)(2,1)} %param.7), channel_id=1, source_target_pairs={{0,24},{8,0},{16,8},{24,16},{1,25},{9,1},{17,9},{25,17},{2,26},{10... | collective-permute-start | bytes 3538952 | tf_op jit(solution)/shard_map/ppermute | solution.py:106
  11.1 25.5 %collective-permute-done = bf16[4608,128]{1,0:T(8,128)(2,1)S(1)} collective-permute-done((bf16[4608,128]{1,0:T(8,128)(2,1)}, bf16[4608,128]{1,0:T(8,128)(2,1)S(1)}, u32[]{:S(2)}, u32[]{:S(2)}) %collective-permute-start) | collective-permute-done | bytes 1179680 | tf_op jit(solution)/shard_map/ppermute | solution.py:106
  36.7 2.9 pad_maximum_fusion.1
  44.3 2.6 fusion.29
  46.8 4.9 %all-to-all-start = ((bf16[1,8,64,512]{3,2,0,1:T(8,128)(2,1)}), bf16[1,8,64,512]{3,2,0,1:T(8,128)(2,1)S(1)}, u32[]{:S(2)}, u32[]{:S(2)}) async-start(bf16[1,8,64,512]{3,2,0,1:T(8,128)(2,1)} %fusion.29), calls=%async_computation | async-start | bytes 1048576 | tf_op jit(solution)/shard_map/all_to_all | solution.py:123
  53.1 2.9 pad_slice_fusion.7
  56.0 2.0 copy.46
  58.0 2.1 copy.45
  60.1 2.1 copy.44
  62.1 2.0 copy.43
  64.2 2.1 copy.42
  66.2 2.1 copy.41
  68.3 2.1 copy.40
  70.4 2.0 copy.39
  73.2 18.8 %collective-permute-done.1 = bf16[4608,256]{1,0:T(8,128)(2,1)} collective-permute-done((bf16[4608,256]{1,0:T(8,128)(2,1)}, bf16[4608,256]{1,0:T(8,128)(2,1)}, u32[]{:S(2)}, u32[]{:S(2)}) %collective-permute-start.1) | collective-permute-done | bytes 2359328 | tf_op jit(solution)/shard_map/ppermute | solution.py:106
  92.1 2.0 constant_dynamic-update-slice_fusion.3
  94.9 2.0 constant_dynamic-update-slice_fusion
  105.7 1.8 copy.58
  108.0 5.7 %reduce.16 = bf16[512,512]{1,0:T(8,128)(2,1)} reduce(bf16[512,1,1,512]{3,2,1,0:T(2,128)(2,1)} %bitcast.222, bf16[]{:T(256)} %broadcast.544), dimensions={1,2}, to_apply=%bitcast.196.reduce_sub_computation | reduce | bytes 1048578
  113.8 2.2 reshape.596
  116.0 20.3 %all_to_all.21 = bf16[8,2,16384]{2,1,0:T(2,128)(2,1)} all-to-all(bf16[8,2,16384]{2,1,0:T(2,128)(2,1)} %reshape.596), channel_id=1, replica_groups=mesh['dp'=4,'wide'=8] {'wide'}, dimensions={0} | all-to-all | bytes 1048576 | tf_op jit(solution)/shard_map/all_to_all | solution.py:117
  136.3 3.5 reshape.597
  142.5 1.9 pad_maximum_fusion
  144.5 3.7 %copy.53 = f32[1536,512]{0,1:T(8,128)} copy(f32[1536,512]{1,0:T(8,128)} %pad_maximum_fusion) | data formatting | bytes 6291456
  163.1 9.7 %copy.51 = f32[4608,512]{0,1:T(8,128)} copy(f32[4608,512]{1,0:T(8,128)} %fusion) | data formatting | bytes 18874368
  172.8 15.7 %reduce-scatter.15.cloned.1.call-done = f32[64,1536]{1,0:T(8,128)} async-done(((f32[512,1536]{1,0:T(8,128)}), f32[64,1536]{1,0:T(8,128)}) %reduce-scatter.15.cloned.1.call-update) | async-done | bytes 393232
  188.5 2.1 copy.54
  194.7 94.9 %reduce-scatter.13.cloned.1.call-done = f32[64,4608]{1,0:T(8,128)} async-done(((f32[512,4608]{1,0:T(8,128)}), f32[64,4608]{1,0:T(8,128)}) %reduce-scatter.13.cloned.1.call-update) | async-done | bytes 1179664
  289.6 2.9 copy.52
  303.8 2.6 fusion.26
  306.4 10.7 %reduce-scatter.11.cloned.1.call-done = f32[384,64]{1,0:T(8,128)} async-done(((f32[1536,64]{1,0:T(8,128)}), f32[384,64]{1,0:T(8,128)}) %reduce-scatter.11.cloned.1.call-update) | async-done | bytes 98320 | tf_op jit(solution)/shard_map/reduce_scatter | solution.py:143
  318.8 38.6 %reduce-scatter.9.cloned.1.call-done = f32[1152,64]{1,0:T(8,128)} async-done(((f32[4608,64]{1,0:T(8,128)}), f32[1152,64]{1,0:T(8,128)}) %reduce-scatter.9.cloned.1.call-update) | async-done | bytes 294928 | tf_op jit(solution)/shard_map/reduce_scatter | solution.py:142
  (110 shorter events, 53.2 us)
Async XLA Ops:
  7.2 29.5 %collective-permute-start = (bf16[4608,128]{1,0:T(8,128)(2,1)}, bf16[4608,128]{1,0:T(8,128)(2,1)S(1)}, u32[]{:S(2)}, u32[]{:S(2)}) collective-permute-start(bf16[4608,128]{1,0:T(8,128)(2,1)} %param.7), channel_id=1, source_target_pairs={{0,24},{8,0},{16,8},{24,16},{1,25},{9,1},{17,9},{25,17},{2,26},{10... | collective-permute-start | bytes 3538952 | tf_op jit(solution)/shard_map/ppermute | solution.py:106
  39.6 52.4 %collective-permute-start.1 = (bf16[4608,256]{1,0:T(8,128)(2,1)}, bf16[4608,256]{1,0:T(8,128)(2,1)}, u32[]{:S(2)}, u32[]{:S(2)}) collective-permute-start(bf16[4608,256]{1,0:T(8,128)(2,1)} %pad_maximum_fusion.1), channel_id=1, source_target_pairs={{0,16},{8,24},{16,0},{24,8},{1,17},{9,25},{17,1},{25,9},{2,18},{10... | collective-permute-start | bytes 7077896 | tf_op jit(solution)/shard_map/ppermute | solution.py:106
  44.3 28.2 %copy-start.1 = (bf16[4608,128]{1,0:T(8,128)(2,1)S(1)}, bf16[4608,128]{1,0:T(8,128)(2,1)}, u32[]{:S(2)}) copy-start(bf16[4608,128]{1,0:T(8,128)(2,1)} %param.7) | copy-start | bytes 3538948
  46.8 55.7 %all-to-all-start = ((bf16[1,8,64,512]{3,2,0,1:T(8,128)(2,1)}), bf16[1,8,64,512]{3,2,0,1:T(8,128)(2,1)S(1)}, u32[]{:S(2)}, u32[]{:S(2)}) async-start(bf16[1,8,64,512]{3,2,0,1:T(8,128)(2,1)} %fusion.29), calls=%async_computation | async-start | bytes 1048576 | tf_op jit(solution)/shard_map/all_to_all | solution.py:123
  51.7 136.8 %reduce-scatter.15.cloned.1.call-start = ((), (), s32[]{:S(2)}) async-start(), calls=%async_computation.9 | async-start | bytes 3538944
  72.4 24.6 %copy-start.7 = (bf16[1,4,128,512]{3,2,1,0:T(8,128)(2,1)S(1)}, bf16[1,4,128,512]{3,2,1,0:T(8,128)(2,1)}, u32[]{:S(2)}) copy-start(bf16[1,4,128,512]{3,2,1,0:T(8,128)(2,1)} %copy.46) | copy-start | bytes 1572868
  72.8 24.7 %copy-start.8 = (bf16[1,4,128,512]{3,2,1,0:T(8,128)(2,1)S(1)}, bf16[1,4,128,512]{3,2,1,0:T(8,128)(2,1)}, u32[]{:S(2)}) copy-start(bf16[1,4,128,512]{3,2,1,0:T(8,128)(2,1)} %copy.45) | copy-start | bytes 1572868
  73.2 24.7 %copy-start.9 = (bf16[1,4,128,512]{3,2,1,0:T(8,128)(2,1)S(1)}, bf16[1,4,128,512]{3,2,1,0:T(8,128)(2,1)}, u32[]{:S(2)}) copy-start(bf16[1,4,128,512]{3,2,1,0:T(8,128)(2,1)} %copy.44) | copy-start | bytes 1572868
  73.2 25.2 %copy-start.10 = (bf16[1,4,128,512]{3,2,1,0:T(8,128)(2,1)S(1)}, bf16[1,4,128,512]{3,2,1,0:T(8,128)(2,1)}, u32[]{:S(2)}) copy-start(bf16[1,4,128,512]{3,2,1,0:T(8,128)(2,1)} %copy.43) | copy-start | bytes 1572868
  94.1 4.8 %copy-start.3 = (bf16[1,1,4,128,512]{4,3,2,1,0:T(8,128)(2,1)S(1)}, bf16[1,1,4,128,512]{4,3,2,1,0:T(8,128)(2,1)}, u32[]{:S(2)}) copy-start(bf16[1,1,4,128,512]{4,3,2,1,0:T(8,128)(2,1)} %param.6) | copy-start | bytes 1572868
  94.1 5.3 %copy-start.11 = (bf16[1,4,128,512]{3,2,1,0:T(8,128)(2,1)S(1)}, bf16[1,4,128,512]{3,2,1,0:T(8,128)(2,1)}, u32[]{:S(2)}) copy-start(bf16[1,4,128,512]{3,2,1,0:T(8,128)(2,1)} %copy.42) | copy-start | bytes 1572868
  94.5 5.3 %copy-start.12 = (bf16[1,4,128,512]{3,2,1,0:T(8,128)(2,1)S(1)}, bf16[1,4,128,512]{3,2,1,0:T(8,128)(2,1)}, u32[]{:S(2)}) copy-start(bf16[1,4,128,512]{3,2,1,0:T(8,128)(2,1)} %copy.41) | copy-start | bytes 1572868
  94.9 5.3 %copy-start.13 = (bf16[1,4,128,512]{3,2,1,0:T(8,128)(2,1)S(1)}, bf16[1,4,128,512]{3,2,1,0:T(8,128)(2,1)}, u32[]{:S(2)}) copy-start(bf16[1,4,128,512]{3,2,1,0:T(8,128)(2,1)} %copy.40) | copy-start | bytes 1572868
  97.0 4.6 %copy-start = (bf16[4608,1024]{1,0:T(8,128)(2,1)}, bf16[4608,1024]{1,0:T(8,128)(2,1)S(1)}, u32[]{:S(2)}) copy-start(bf16[4608,1024]{1,0:T(8,128)(2,1)S(1)} %constant_dynamic-update-slice_fusion) | copy-start | bytes 28311556
  97.0 3.7 %copy-start.5 = (bf16[1,4,128,512]{3,2,1,0:T(8,128)(2,1)S(1)}, bf16[1,4,128,512]{3,2,1,0:T(8,128)(2,1)}, u32[]{:S(2)}) copy-start(bf16[1,4,128,512]{3,2,1,0:T(8,128)(2,1)} %copy.39) | copy-start | bytes 1572868
  99.3 3.2 copy-start.14
  99.3 3.2 copy-start.15
  101.6 39.5 %copy-start.2 = (bf16[1,8,64,512]{3,2,1,0:T(8,128)(2,1)S(1)}, bf16[1,8,64,512]{3,2,1,0:T(8,128)(2,1)}, u32[]{:S(2)}) copy-start(bf16[1,8,64,512]{3,2,1,0:T(8,128)(2,1)} %param.11) | copy-start | bytes 1572868
  144.5 11.2 %copy-start.4 = (bf16[1,1,4,128,512]{4,3,2,1,0:T(8,128)(2,1)S(1)}, bf16[1,1,4,128,512]{4,3,2,1,0:T(8,128)(2,1)}, u32[]{:S(2)}) copy-start(bf16[1,1,4,128,512]{4,3,2,1,0:T(8,128)(2,1)} %param.6) | copy-start | bytes 1572868
  148.2 141.4 %reduce-scatter.13.cloned.1.call-start = ((), (), s32[]{:S(2)}) async-start(), calls=%async_computation.8 | async-start | bytes 10616832
  172.8 144.4 %reduce-scatter.11.cloned.1.call-start = ((), (), s32[]{:S(2)}) async-start(), calls=%async_computation.7 | async-start | bytes 983040 | tf_op jit(solution)/shard_map/reduce_scatter | solution.py:143
  190.7 166.7 %reduce-scatter.9.cloned.1.call-start = ((), (), s32[]{:S(2)}) async-start(), calls=%async_computation.6 | async-start | bytes 2949120 | tf_op jit(solution)/shard_map/reduce_scatter | solution.py:142
  194.6 104.5 %copy-start.6 = (bf16[1,4,128,512]{3,2,1,0:T(8,128)(2,1)S(1)}, bf16[1,4,128,512]{3,2,1,0:T(8,128)(2,1)}, u32[]{:S(2)}) copy-start(bf16[1,4,128,512]{3,2,1,0:T(8,128)(2,1)} %get-tuple-element.23) | copy-start | bytes 1572868
Sparse Core Ops, SparseCore 0:
  148.3 40.1 reduce-scatter.14
  190.8 98.6 reduce-scatter.12
  292.5 24.6 reduce-scatter.10
  320.0 37.3 reduce-scatter.8
